TPU v7x, 32 devices: a whole 2x2x4 slice. The times are simulated.
32 devices in a mesh: region: 4 (over y, x), col: 8 (over z, core).
Axes of the slice: x: 2, y: 2, z: 4, core: 2. Of those that a mesh axis runs over, the one named last changes fastest.
Arguments:
- jac: bfloat16 [256, 128], P(('region', 'col')), may hold values from -2 to 2
- dest: int32 [256, 2], P(('region', 'col')), may hold values from 0 to 3, all different within a row; in each aligned block of 8 rows (0 to 7, 8 to 15, ...) at most 6 rows name the same one
- near_pose: int32 [256, 2], P(('region', 'col')), may hold values from 0 to 255
- prior: float32 [8192], P('region'), may hold values from 0.5 to 8
Outputs:
- front_out: float32 [8192, 8192], P('region', 'col')
Inputs may be any that keep to these rules, and one draw needn't show every extreme that they name: `dest`: each row names two different regions; among the 8 rows of one device no region is named more than 6 times, and in some device's rows some region is named exactly 6 times.
All inputs are finite; a program needn't handle non-finite values.
Results may differ from a plain program's by a relative error of at most 0.00045.
Values may be sent and summed in bfloat16 or wider, within the bound.
No kernel may reach another device: no remote copies, remote signals or barrier semaphores. Data moves between devices by JAX's collectives and lax.ppermute only.
A program may use at most 320 MiB of HBM per device.

v0:
```python
import functools

import jax
import jax.numpy as jnp
from jax import lax
from jax.experimental import pallas as pl
from jax.experimental.pallas import tpu as pltpu
from jax.sharding import PartitionSpec as P

NB = 128
K_PANELS = 2
PANEL = NB * K_PANELS
PP = PANEL // 8
CH = 256
BIG = float(1 << 24)
f32, bf16, i32 = jnp.float32, jnp.bfloat16, jnp.int32


def iota(shape, dim):
    return lax.broadcasted_iota(i32, shape, dim)


def split(x, parts):
    out = []
    for _ in range(parts):
        top = x.astype(bf16)
        out.append(top)
        x = x - top.astype(f32)
    return out


def dot(a, b, dims=((1,), (0,))):
    return lax.dot_general(a, b, (dims, ((), ())), preferred_element_type=f32)


SLOT = 10


def pack_kernel(place, jac_ref, dest_ref, near_ref, prior_ref, out_ref):
    _, column = place()
    lane = iota((1, 128), 1)
    fill_up = jnp.zeros((2, 120), f32)
    dest = jnp.concatenate([dest_ref[...].astype(f32), fill_up], axis=1)
    near = jnp.concatenate([near_ref[...].astype(f32), fill_up], axis=1)
    line = dest[0:1, :] + pltpu.roll(near[0:1, :], 8, 1)
    line = line + pltpu.roll(dest[1:2, :], 16, 1) + pltpu.roll(near[1:2, :], 24, 1)
    column = column % 8
    prior = prior_ref[pl.ds(column // 4, 1), :]
    prior = pltpu.roll(prior, (4 - column % 4) % 4 * 32, 1)
    for at, part in enumerate(split(prior, 3)):
        moved = pltpu.roll(part.astype(f32), 32 * (at + 1), 1)
        line = jnp.where(lane // 32 == at + 1, moved, line)
    slot = jnp.concatenate([jac_ref[...].astype(f32), line, jnp.zeros((1, 128), f32)], axis=0)
    eight = jnp.concatenate([slot] * 8, axis=0).astype(bf16)
    for at in range(out_ref.shape[0] // (8 * SLOT)):
        out_ref[8 * SLOT * at : 8 * SLOT * (at + 1), :] = eight


def pack(place, jac, dest, near_pose, prior2, devices):
    return pl.pallas_call(
        functools.partial(pack_kernel, place),
        out_shape=jax.ShapeDtypeStruct((devices * SLOT, 128), bf16),
        in_specs=[pl.BlockSpec(memory_space=pltpu.VMEM)] * 4,
        out_specs=pl.BlockSpec(memory_space=pltpu.VMEM),
        name="pack",
    )(jac, dest.T, near_pose.T, prior2)


def fill_kernel(place, sizes, prior_ref, out_ref, zeros, squares, sem, sem2):
    rows, cols = sizes
    region, column = place()
    pieces = rows // zeros.shape[0]
    zeros[...] = jnp.zeros_like(zeros)
    step = zeros.shape[0]
    copies = [
        pltpu.make_async_copy(zeros, out_ref.at[pl.ds(at * step, step), :], sem.at[at])
        for at in range(pieces)
    ]
    for copy in copies:
        copy.start()
    start = column * cols - region * rows
    own = (start >= 0) & (start < rows)

    @pl.when(own)
    def _():
        diagonal = iota((128, 128), 0) == iota((128, 128), 1)
        first = start // 128
        for at in range(cols // 128):
            squares[at] = jnp.where(diagonal, prior_ref[pl.ds(first + at, 1), :], 0.0)

    for copy in copies:
        copy.wait()

    @pl.when(own)
    def _():
        base = pl.multiple_of(start, 128)
        patches = [
            pltpu.make_async_copy(
                squares.at[at],
                out_ref.at[pl.ds(base + at * 128, 128), pl.ds(at * 128, 128)],
                sem2.at[at],
            )
            for at in range(cols // 128)
        ]
        for patch in patches:
            patch.start()
        for patch in patches:
            patch.wait()


def fill(place, rows, cols, prior2):
    step = min(256, rows)
    return pl.pallas_call(
        functools.partial(fill_kernel, place, (rows, cols)),
        out_shape=jax.ShapeDtypeStruct((rows, cols), f32),
        out_specs=pl.BlockSpec(memory_space=pl.ANY),
        scratch_shapes=[
            pltpu.VMEM((step, cols), f32),
            pltpu.VMEM((cols // 128, 128, 128), f32),
            pltpu.SemaphoreType.DMA((rows // step,)),
            pltpu.SemaphoreType.DMA((cols // 128,)),
        ],
        cost_estimate=pl.CostEstimate(flops=0, bytes_accessed=rows * cols * 4, transcendentals=0),
        name="fill",
    )(prior2)


def batched(left, right):
    out = []
    for k in range(8):
        total = left[0][k : k + 1, :] * right[0]
        for e in range(1, 8):
            total = total + left[e][k : k + 1, :] * right[e]
        out.append(total)
    return out


def slabs(block):
    return [block[8 * e : 8 * e + 8, :] for e in range(8)]


def to_columns(rows):
    full = jnp.concatenate([rows, jnp.zeros((120, CH), f32)], axis=0)
    return full.T


def cholesky(a):
    row = iota((8, 128), 0)
    columns, scales = [], []
    a = list(a)
    for j in range(8):
        pivot = a[j][j : j + 1, :]
        scale = lax.rsqrt(pivot)
        scale = scale * (1.5 - 0.5 * pivot * scale * scale)
        column = jnp.where(row >= j, a[j] * scale, 0.0)
        for k in range(j + 1, 8):
            a[k] = a[k] - column * column[k : k + 1, :]
        columns.append(column)
        scales.append(scale)
    inverse = []
    for i in range(8):
        x = jnp.where(row == i, 1.0, 0.0)
        for j in range(i, 8):
            value = x[j : j + 1, :] * scales[j]
            x = jnp.where(row == j, value, jnp.where(row > j, x - columns[j] * value, x))
        inverse.append(x)
    return columns, inverse


def loop(count, body):
    if count == 1:
        body(0)
    else:
        lax.fori_loop(0, count, lambda at, carry: (body(at), carry)[1], 0)


def expansion():
    row, lane = iota((8, 128), 0), iota((8, 128), 1)
    none = jnp.zeros((8, 128), f32)
    straight = jnp.where(lane % 8 == row, 1.0, 0.0)
    by_rows = [
        jnp.concatenate([straight if at == k else none for at in range(8)], axis=1)
        for k in range(8)
    ]
    by_columns = [
        jnp.concatenate(
            [jnp.where((row == at) & (lane % 8 == j), 1.0, 0.0) for at in range(8)], axis=1
        )
        for j in range(8)
    ]
    return jnp.concatenate((by_rows + by_columns) * 2, axis=0).astype(bf16)


def label_rows(got_ref, a):
    per = CH // 8
    block = got_ref[pl.ds(a * per * SLOT, per * SLOT), :].astype(f32)
    return jnp.concatenate([block[SLOT * d + 8 : SLOT * d + 9, :] for d in range(per)], axis=0)


def jac_columns(got_ref, a):
    per = CH // 8
    block = got_ref[pl.ds(a * per * SLOT, per * SLOT), :].astype(f32)
    return jnp.concatenate([block[SLOT * d : SLOT * d + 8, :] for d in range(per)], axis=0).T


def spread(labels):
    lane8, row8 = iota((8, 128), 1), iota((8, 128), 0)
    out = []
    for at in range(4):
        halves = []
        for half in range(2):
            total = jnp.zeros((8, 128), f32)
            for part in range(2):
                from_row = 16 * half + 8 * part
                piece = labels[from_row : from_row + 8, :]
                if at:
                    piece = pltpu.roll(piece, 128 - 8 * at, 1)
                piece = pltpu.roll(piece, 64 * part, 1, stride=8, stride_axis=0)
                total = total + jnp.where(lane8 // 8 == row8 + 8 * part, piece, 0.0)
            halves.append(jnp.sum(total, axis=0, keepdims=True))
        out.append(jnp.concatenate(halves, axis=1))
    return out


def on_diagonal(prior_row):
    kl, unknown = iota((64, PANEL), 0), iota((64, PANEL), 1)
    diagonal = jnp.where((kl // 8 == kl % 8) & (unknown % 8 == kl % 8), prior_row, 0.0)
    own_pose = jnp.where(iota((PANEL, 128), 0) // 8 == iota((PANEL, 128), 1), 1.0, 0.0).astype(bf16)
    first = dot(jnp.concatenate(split(diagonal, 3), axis=0), own_pose)
    kl = iota((64, 128), 0)
    spare = (kl // 8 == kl % 8) & (iota((64, 128), 1) >= PP)
    return first[0:64] + first[64:128] + first[128:192] + jnp.where(spare, 1.0, 0.0)


def first_region(place, sizes, got_ref, prior_ref, out_ref, app, squares, sem):
    rows, cols, chunks = sizes
    col_poses, groups = cols // 8, cols // 128
    _, column = place()
    column_f = column.astype(f32)
    start = pl.multiple_of(column * cols, 128)
    local = prior_ref[pl.ds(column * groups, groups), :]
    prior_row = jnp.concatenate([prior_ref[0:1, :], prior_ref[1:2, :]], axis=1)
    first = on_diagonal(prior_row)
    app[...] = jnp.zeros_like(app)

    def measure(a):
        jac_t = jac_columns(got_ref, a)
        d0, n0, d1, n1 = spread(label_rows(got_ref, a))
        here0 = d0 == 0
        pose = jnp.where(here0, n0, n1) - column_f * col_poses
        inside = (here0 | (d1 == 0)) & (pose >= 0) & (pose < col_poses)
        pose = jnp.where(inside, pose, -1.0)
        columns = to_columns(jnp.concatenate([pose, jnp.zeros((7, CH), f32)], axis=0))
        j0, j1 = slabs(jac_t[0:64, :]), slabs(jac_t[64:128, :])
        side = [jnp.where(here0, x, y) for x, y in zip(j0, j1)]
        gram = jnp.concatenate(batched(side, side), axis=0)
        of_pose = jnp.where(
            columns[:, 0:1] == iota((CH, 128), 1).astype(f32), 1.0, 0.0
        ).astype(bf16)
        total = dot(jnp.concatenate(split(gram, 3), axis=0), of_pose)
        app[...] += total[0:64] + total[64:128] + total[128:192]

    loop(chunks, measure)
    gram = app[...]
    factor, _ = cholesky(slabs(gram + first))
    lane, here = iota((64, 128), 1), jnp.where(column == 0, PP, 0)
    in_panel = lane < here
    both = [jnp.where(in_panel, 0.0, gram), jnp.where(in_panel, jnp.concatenate(factor, axis=0), 0.0)]
    both = jnp.concatenate(both, axis=0).T
    value = dot(jnp.concatenate(split(both, 2), axis=1), expansion())
    pose, lane = iota((128, 128), 0), iota((128, 128), 1)
    weights = [jnp.broadcast_to(local[at : at + 1, :], (16, 128)) for at in range(groups)]
    weights += [jnp.zeros((16, 128), f32)] * (8 - groups)
    weights = jnp.where(pose < here, 0.0, jnp.concatenate(weights, axis=0))
    keep, lane_in, group_lane = lane // 8 == pose % 16, lane % 8, lane // 8
    for k in range(8):
        piece = jnp.where(keep, value[:, 128 * k : 128 * k + 128], 0.0)
        piece = piece + jnp.where(keep & (lane_in == k), weights, 0.0)
        squares[pl.ds(k, 128, stride=8), :] = piece
    copies = [
        pltpu.make_async_copy(
            squares.at[pl.ds(at * 128, 128), :],
            out_ref.at[pl.ds(start + at * 128, 128), pl.ds(at * 128, 128)],
            sem.at[at],
        )
        for at in range(groups)
    ]
    for copy in copies:
        copy.start()
    for copy in copies:
        copy.wait()


def general(place, sizes, got_ref, prior_ref, out_ref,
                    jt, rows_s, cols_s, app, bt, blk, tiles, keys,
                    listing, info, list_sm, info_sm, extra_sm, sem_list, sem_info, sem_out):
    rows, cols, chunks = sizes
    row_poses, col_poses, groups = rows // 8, cols // 8, cols // 128
    region, column = place()
    region_f, column_f = region.astype(f32), column.astype(f32)
    start = column * cols - region * rows
    own = (start >= 0) & (start < rows)
    share = jnp.where(own, 1.0, 0.0)
    lane8, row8 = iota((8, 128), 1), iota((8, 128), 0)
    before = iota((CH, CH), 0) < iota((CH, CH), 1)
    table = expansion()

    labels0 = label_rows(got_ref, 0)
    sent = labels0[0:8, :]
    panel_prior = jnp.zeros((8, 128), f32)
    for at in range(3):
        panel_prior = panel_prior + pltpu.roll(sent, 128 - 32 * (at + 1), 1)
    panel_prior = jnp.where(lane8 < 32, panel_prior, 0.0)
    lined = jnp.zeros((8, 128), f32)
    for at in range(4):
        moved = panel_prior if at == 0 else pltpu.roll(panel_prior, 32 * at, 1)
        lined = lined + jnp.where(row8 % 4 == at, moved, 0.0)
    halves = [
        jnp.sum(jnp.where(row8 < 4, lined, 0.0), axis=0, keepdims=True),
        jnp.sum(jnp.where(row8 >= 4, lined, 0.0), axis=0, keepdims=True),
    ]
    prior_row = jnp.concatenate(halves, axis=1)
    app[...] = on_diagonal(prior_row)

    def measure(a):
        jac_t = jac_columns(got_ref, a)
        jt[a] = jac_t
        d0, n0, d1, n1 = spread(labels0 if chunks == 1 else label_rows(got_ref, a))
        c0 = d0 * row_poses + n0 - column_f * col_poses
        c1 = d1 * row_poses + n1 - column_f * col_poses
        one, none = jnp.ones_like(d0), jnp.zeros_like(d0)
        row0, row1 = d0 == region_f, d1 == region_f
        col0, col1 = (c0 >= 0) & (c0 < col_poses), (c1 >= 0) & (c1 < col_poses)
        pan0, pan1 = (d0 == 0) & (n0 < PP), (d1 == 0) & (n1 < PP)
        has_row = jnp.where(row0 | row1, one, none)
        has_col = jnp.where(col0 | col1, one, none)
        touches = jnp.where(pan0 | pan1, one, none)
        row_pose = jnp.where(row0, n0, n1)
        col_pose = jnp.where(col0, c0, c1)
        pan_side = jnp.where(pan0, none, one)
        pan_pose = jnp.where(pan0, n0, n1)
        row_in_panel = jnp.where((row0 & pan0) | (row1 & pan1), one, none)
        col_in_panel = jnp.where((col0 & pan0) | (col1 & pan1), one, none)
        relevant = has_row * has_col * (1.0 - row_in_panel)
        group = jnp.floor(col_pose * (1.0 / 16.0))
        tile = row_pose * groups + group
        cell = row_pose * col_poses + col_pose
        is_row = touches * has_row * (1.0 - row_in_panel)
        is_col = touches * has_col * (1.0 - col_in_panel)
        lines = [
            jnp.where(relevant > 0, tile, -1.0),
            jnp.where(relevant > 0, cell, -1.0),
            jnp.where(touches > 0, pan_pose, -1.0),
            jnp.where(is_row > 0, pan_pose, -1.0),
            col_pose - group * 16.0,
            none, none, none,
        ]
        more = [
            jnp.where(relevant > 0, tile, -2.0),
            jnp.where(relevant > 0, cell, -2.0),
            jnp.where(is_col > 0, pan_pose, -2.0),
            relevant,
            row_pose,
            group,
            col_pose,
            is_row * is_col,
            jnp.where(row0, none, one),
            jnp.where(col0, none, one),
            pan_side,
            col_in_panel,
            none, none, none, none,
        ]
        lines = jnp.concatenate(lines, axis=0)
        rows_s[a] = jnp.concatenate([lines] + more, axis=0)
        columns = to_columns(lines)
        cols_s[a] = columns
        j0, j1 = slabs(jac_t[0:64, :]), slabs(jac_t[64:128, :])
        near = [jnp.where(pan_side == 0, x, y) for x, y in zip(j0, j1)]
        gram = jnp.concatenate(batched(near, near), axis=0)
        of_pose = jnp.where(
            columns[:, 2:3] == iota((CH, 128), 1).astype(f32), 1.0, 0.0
        ).astype(bf16)
        total = dot(jnp.concatenate(split(gram, 3), axis=0), of_pose)
        app[...] += total[0:64] + total[64:128] + total[128:192]

    loop(chunks, measure)

    def earlier_of(a, at, at_right):
        def from_chunk(b, count):
            other = jnp.broadcast_to(cols_s[b, :, at : at + 1], (CH, CH))
            same = jnp.where(other == rows_s[a, at_right : at_right + 1, :], 1.0, 0.0)
            if chunks == 1:
                same = jnp.where(before, same, 0.0)
            else:
                here, all_of_it = jnp.where(b == a, 1.0, 0.0), jnp.where(b < a, 1.0, 0.0)
                same = jnp.where(before, same, 0.0) * here + same * all_of_it
            return count + jnp.sum(same, axis=0, keepdims=True)

        nothing = jnp.zeros((1, CH), f32)
        return from_chunk(0, nothing) if chunks == 1 else lax.fori_loop(0, chunks, from_chunk, nothing)

    def lists(a):
        relevant = rows_s[a, 11:12, :]
        kept = jnp.where(earlier_of(a, 0, 8) == 0, relevant, 0.0)
        lone = jnp.where(earlier_of(a, 1, 9) == 0, relevant, 0.0)
        joins = lone * (1.0 - kept)
        rows_s[a, 20:21, :] = kept
        count = jnp.sum(kept, axis=1, keepdims=True)
        upper = jnp.where(before, 1.0, 0.0).astype(bf16)
        rank = dot(jnp.broadcast_to(kept, (16, CH)).astype(bf16), upper)[0:1, :]
        slot = iota((CH, CH), 0)
        slot = (slot % 64 * 4 + slot // 64).astype(f32)
        slot = jnp.where(slot < count, slot, 0.0)
        chosen = jnp.where((rank == slot) & (kept > 0), 1.0, 0.0).astype(bf16)
        position = iota((1, CH), 1).astype(f32)
        data = jnp.concatenate(
            [rows_s[a, 12:13, :], rows_s[a, 13:14, :], position, jnp.zeros((13, CH), f32)], axis=0
        ).astype(bf16)
        found = dot(data, chosen, ((1,), (1,)))[0:8, :]
        code = found[2:3, :] + found[0:1, :] * 256.0 + found[1:2, :] * 65536.0
        line = [code[:, 0:128], pltpu.roll(code[:, 0:128], 64, 1)]
        line += [code[:, 128:256], pltpu.roll(code[:, 128:256], 64, 1)]
        line += [jnp.broadcast_to(count, (1, 128)), jnp.zeros((3, 128), f32)]
        listing[a] = jnp.concatenate(line, axis=0).astype(i32)
        pltpu.make_async_copy(listing.at[a], list_sm.at[a], sem_list.at[a]).start()
        info[a] = jnp.concatenate(
            [rows_s[a, 12:13, :], rows_s[a, 14:15, :], joins, jnp.zeros((5, CH), f32)], axis=0
        ).astype(i32)
        pltpu.make_async_copy(info.at[a], info_sm.at[a], sem_info.at[a]).start()

    loop(chunks, lists)

    def key_table(a, b):
        left = jnp.broadcast_to(cols_s[a, :, 3:4], (CH, CH))
        valid = jnp.where(left == rows_s[b, 10:11, :], 1.0, 0.0)
        same = iota((CH, CH), 0) == iota((CH, CH), 1)
        joins = info[a, 2:3, :].astype(f32)
        if chunks > 1:
            flag = jnp.where(a == b, 1.0, 0.0)
            joins = joins * flag + valid * (1.0 - flag)
        valid = jnp.where(same, joins, valid)
        key = (iota((CH, CH), 0) * CH + iota((CH, CH), 1)).astype(f32)
        key = jnp.where(valid > 0, key, BIG)
        keys[...] = key
        return jnp.min(key)

    early = key_table(0, 0) if chunks == 1 else None

    _, inverse = cholesky(slabs(app[...]))
    inverse = jnp.concatenate(split(jnp.concatenate(inverse, axis=0), 3), axis=0)

    def blocks(a):
        row = [rows_s[a, at : at + 1, :] for at in range(24)]
        jac_t = jt[a]
        j0, j1 = slabs(jac_t[0:64, :]), slabs(jac_t[64:128, :])
        left = [jnp.where(row[16] == 0, x, y) for x, y in zip(j0, j1)]
        right = [jnp.where(row[17] == 0, x, y) for x, y in zip(j0, j1)]
        near = [jnp.where(row[18] == 0, x, y) for x, y in zip(j0, j1)]
        far = [jnp.where(row[18] == 0, y, x) for x, y in zip(j0, j1)]
        gram = batched(left, right)
        cross = batched(near, far)
        of_pose = jnp.where(iota((128, CH), 0).astype(f32) == row[2], 1.0, 0.0).astype(bf16)
        inv = dot(inverse, of_pose)
        inv = slabs(inv[0:64] + inv[64:128] + inv[128:192])
        solved = []
        for j in range(8):
            total = inv[0][j : j + 1, :] * cross[0]
            for i in range(1, j + 1):
                total = total + inv[i][j : j + 1, :] * cross[i]
            solved.append(total)
        bt[a] = jnp.concatenate(solved, axis=0)
        outer = batched(solved, solved)
        keep_normal = row[11] * (1.0 - row[19])
        keep_panel = row[11] * row[19]
        values = [(g - o * row[15]) * keep_normal for g, o in zip(gram, outer)]
        values += [x * keep_panel for x in solved]
        values = jnp.concatenate(values, axis=0)
        high, low = split(values, 2)
        blk[a] = jnp.concatenate([high, low], axis=0)

    loop(chunks, blocks)

    def merge(a):
        line = [rows_s[a, at : at + 1, :] for at in range(24)]

        def from_chunk(b, total):
            other = jnp.broadcast_to(cols_s[b, :, 1:2], (CH, CH))
            same = jnp.where(other == line[9], 1.0, 0.0).astype(bf16)
            found = dot(blk[b], same)
            return total + found[0:128] + found[128:256]

        total = jnp.zeros((128, CH), f32)
        total = from_chunk(0, total) if chunks == 1 else lax.fori_loop(0, chunks, from_chunk, total)
        sixteenth = jnp.floor(line[12] * (1.0 / 16.0))
        pieces = rows // 128
        local = jnp.concatenate(
            [prior_ref[...], jnp.zeros((16 - pieces, 128), f32)], axis=0
        ) if pieces < 16 else prior_ref[...]
        steps = local.shape[0]
        parts = jnp.concatenate(split(local, 3), axis=0)
        of_row = jnp.where(
            (iota((3 * steps, CH), 0) % steps).astype(f32) == sixteenth, 1.0, 0.0
        ).astype(bf16)
        priors = dot(parts, of_row, ((0,), (0,)))
        within = line[12] - sixteenth * 16.0
        on_row = jnp.zeros((8, CH), f32)
        for at in range(16):
            on_row = on_row + jnp.where(within == float(at), priors[8 * at : 8 * at + 8, :], 0.0)
        on_row = on_row * (share * line[11])
        sub = iota((8, CH), 0)
        normal = [
            total[8 * k : 8 * k + 8, :] + jnp.where(sub == k, on_row, 0.0) for k in range(8)
        ]
        total = jnp.concatenate(normal + [total[64:128, :]], axis=0)
        value = dot(jnp.concatenate(split(total.T, 2), axis=1), table)
        keep = (iota((CH, 128), 1) // 8).astype(f32) == cols_s[a, :, 4:5]
        for k in range(8):
            tiles[pl.ds(a * CH * 8 + k, CH, stride=8), :] = jnp.where(
                keep, value[:, 128 * k : 128 * k + 128], 0.0
            )

    loop(chunks, merge)

    def waiting(a):
        pltpu.make_async_copy(listing.at[a], list_sm.at[a], sem_list.at[a]).wait()
        pltpu.make_async_copy(info.at[a], info_sm.at[a], sem_info.at[a]).wait()

    loop(chunks, waiting)
    extra_sm[0] = 0

    def tile_rows(slot, count=1):
        return pl.ds(pl.multiple_of(slot * 8, 8), 8 * count)

    def pairs(index):
        a, b = (0, 0) if chunks == 1 else (index // chunks, index % chunks)

        def one(key_now):
            number = key_now.astype(i32)
            m1, m2 = number >> 8, number & (CH - 1)
            joining = (m1 == m2) if chunks == 1 else ((m1 == m2) & (a == b))
            r1, c2 = info_sm[a, 0, m1], info_sm[b, 1, m2]
            group, within = c2 >> 4, c2 & 15
            code = r1 * groups + group
            code_f = code.astype(f32)
            key_next = jnp.min(jnp.where(keys[...] > key_now, keys[...], BIG))

            def search(chunk, best):
                at_one = (rows_s[chunk, 8:9, :] == code_f) & (rows_s[chunk, 20:21, :] > 0)
                slots = (iota((1, CH), 1) + chunk * CH).astype(f32)
                return jnp.minimum(best, jnp.min(jnp.where(at_one, slots, BIG)))

            slot = search(0, BIG) if chunks == 1 else lax.fori_loop(0, chunks, search, BIG)
            position = iota((8, CH), 1)
            total = jnp.zeros((8, 128), f32)
            for j in range(8):
                x = bt[a, 8 * j : 8 * j + 8, :]
                y = bt[b, 8 * j : 8 * j + 8, :]
                x = jnp.sum(jnp.where(position == m1, x, 0.0), axis=1, keepdims=True)
                y = jnp.sum(jnp.where(position == m2, y, 0.0), axis=1, keepdims=True)
                y = jnp.where(lane8 % 8 == row8, y, 0.0)
                y = jnp.sum(y, axis=0, keepdims=True)
                total = total + x * y
            total = jnp.where(lane8 // 8 == within, -total, 0.0)
            total = jnp.where(joining, tiles[tile_rows(a * CH + m1), :], total)
            added = extra_sm[0]
            slot = jnp.where(slot < BIG, slot, -1.0).astype(i32)

            def at_extra(at, slot):
                return jnp.where(extra_sm[1 + at] == code, chunks * CH + at, slot)

            slot = lax.fori_loop(0, added, at_extra, slot)
            fresh = slot < 0
            slot = jnp.where(fresh, chunks * CH + added, slot)
            where = tile_rows(slot)
            tiles[where, :] = jnp.where(fresh, 0.0, tiles[where, :]) + total

            @pl.when(fresh)
            def _():
                extra_sm[1 + added] = code
                extra_sm[0] = added + 1

            return key_next

        smallest = early if chunks == 1 else key_table(a, b)
        lax.while_loop(lambda key_now: key_now < BIG, one, smallest)

    loop(chunks * chunks, pairs)

    def tile_copy(slot, r, group, count=1):
        return pltpu.make_async_copy(
            tiles.at[tile_rows(slot, count), :],
            out_ref.at[tile_rows(r, count), pl.ds(pl.multiple_of(group * 128, 128), 128)],
            sem_out,
        )

    def send(a):
        def four(at, carry):
            for more in range(4):
                entry = list_sm[a, more, at]
                slot, r = a * CH + (entry & 255), (entry >> 8) & 255
                tile_copy(slot, r, entry >> 16).start()
            return carry
        lax.fori_loop(0, (list_sm[a, 4, 0] + 3) // 4, four, 0)

    loop(chunks, send)

    def send_extra(at, carry):
        code = extra_sm[1 + at]
        tile_copy(chunks * CH + at, code // groups, code % groups).start()
        return carry

    lax.fori_loop(0, extra_sm[0], send_extra, 0)

    def drain_four(at, carry):
        tile_copy(0, 0, 0, 4).wait()
        return carry

    def drain_one(at, carry):
        tile_copy(0, 0, 0).wait()
        return carry

    def drain(a):
        lax.fori_loop(0, (list_sm[a, 4, 0] + 3) // 4, drain_four, 0)

    loop(chunks, drain)
    lax.fori_loop(0, extra_sm[0], drain_one, 0)


def assemble_kernel(place, sizes, got_ref, prior_ref, filled_ref, out_ref,
                    jt, rows_s, cols_s, app, bt, blk, tiles, keys,
                    listing, info, list_sm, info_sm, extra_sm, sem_list, sem_info, sem_out,
                    squares, sem_sq):
    del filled_ref
    rows, cols, _ = sizes
    region, column = place()
    first = (region == 0) & (column * cols < rows)

    @pl.when(first)
    def _():
        first_region(place, sizes, got_ref, prior_ref, out_ref, app, squares, sem_sq)

    @pl.when(jnp.logical_not(first))
    def _():
        general(place, sizes, got_ref, prior_ref, out_ref, jt, rows_s, cols_s, app, bt, blk,
                tiles, keys, listing, info, list_sm, info_sm, extra_sm, sem_list, sem_info, sem_out)


def assemble(place, rows, cols, got, prior2, filled):
    count = got.shape[0] // SLOT * 8
    chunks = count // CH
    capacity = rows // 8 * (cols // 128)
    any_space = pl.BlockSpec(memory_space=pl.ANY)
    vmem = pl.BlockSpec(memory_space=pltpu.VMEM)
    return pl.pallas_call(
        functools.partial(assemble_kernel, place, (rows, cols, chunks)),
        out_shape=jax.ShapeDtypeStruct((rows, cols), f32),
        in_specs=[vmem, vmem, any_space],
        out_specs=any_space,
        scratch_shapes=[
            pltpu.VMEM((chunks, 128, CH), f32),
            pltpu.VMEM((chunks, 24, CH), f32),
            pltpu.VMEM((chunks, CH, 128), f32),
            pltpu.VMEM((64, 128), f32),
            pltpu.VMEM((chunks, 64, CH), f32),
            pltpu.VMEM((chunks, 256, CH), bf16),
            pltpu.VMEM(((count + capacity) * 8, 128), f32),
            pltpu.VMEM((CH, CH), f32),
            pltpu.VMEM((chunks, 8, 128), i32),
            pltpu.VMEM((chunks, 8, CH), i32),
            pltpu.SMEM((chunks, 8, 128), i32),
            pltpu.SMEM((chunks, 8, CH), i32),
            pltpu.SMEM((1 + capacity,), i32),
            pltpu.SemaphoreType.DMA((chunks,)),
            pltpu.SemaphoreType.DMA((chunks,)),
            pltpu.SemaphoreType.DMA,
            pltpu.VMEM((1024, 128), f32),
            pltpu.SemaphoreType.DMA((cols // 128,)),
        ],
        input_output_aliases={2: 0},
        compiler_params=pltpu.CompilerParams(vmem_limit_bytes=48 << 20),
        name="assemble",
    )(got, prior2, filled)


def place():
    return lax.axis_index("region"), lax.axis_index("col")


def body(jac, dest, near_pose, prior):
    regions, columns = lax.axis_size("region"), lax.axis_size("col")
    devices = regions * columns
    rows = prior.shape[0]
    cols = rows * regions // columns
    assert jac.shape[0] == 8 and devices * 8 % CH == 0
    assert rows % cols == 0 and rows // 8 <= 256 and regions <= 256
    assert cols // 8 <= 128 and rows // 8 * (cols // 128) <= 2048
    assert rows >= PANEL and cols >= PANEL and cols % 128 == 0 and columns % 8 == 0
    prior2 = prior.reshape(rows // 128, 128)
    packed = pack(place, jac, dest, near_pose, prior2, devices).reshape(devices, SLOT // 2, 2, 128)
    got = lax.all_to_all(packed, ("region", "col"), split_axis=0, concat_axis=0, tiled=True)
    got = got.reshape(devices * SLOT, 128)
    filled = fill(place, rows, cols, prior2)
    return assemble(place, rows, cols, got, prior2, filled)


def solution(mesh):
    return jax.shard_map(
        body,
        mesh=mesh,
        in_specs=(
            P(("region", "col"), None),
            P(("region", "col"), None),
            P(("region", "col"), None),
            P("region"),
        ),
        out_specs=P("region", "col"),
        check_vma=False,
    )
```

profile of v0, /device:TPU:0, one launch (start us, length us, event | category | flops | bytes accessed | tf_op | source)
XLA Modules:
  0.0 18.3 jit_solution(18410504686288471269)
XLA Ops:
  0.0 0.0 copy-start
  0.0 1.5 %pack.1 = bf16[320,128]{1,0:T(8,128)(2,1)} custom-call(bf16[8,128]{1,0:T(8,128)(2,1)} %jac_ref.1, s32[2,8]{1,0:T(2,128)} %bitcast.10, s32[2,8]{1,0:T(2,128)} %bitcast.11, f32[16,128]{1,0:T(8,128)} %bitcast.6), custom_call_target="tpu_custom_call" | custom-call | tf_op jit(solution)/shard_map/pack/pallas_call | solution.py:60
  1.5 7.3 %all-to-all-start = ((bf16[32,5,2,128]{3,2,1,0:T(2,128)(2,1)}), bf16[32,5,2,128]{3,2,1,0:T(2,128)(2,1)S(1)}, u32[]{:S(2)}, u32[]{:S(2)}) async-start(bf16[32,5,2,128]{3,2,1,0:T(2,128)(2,1)} %bitcast.9), calls=%async_computation | async-start | bytes 163840 | tf_op jit(solution)/shard_map/all_to_all | solution.py:700
  8.9 5.0 %fill.1.filled_ref = f32[2048,1024]{1,0:T(8,128)} custom-call(f32[16,128]{1,0:T(8,128)} %bitcast.7), custom_call_target="tpu_custom_call" | custom-call | bytes 8388608 | tf_op jit(solution)/shard_map/fill/pallas_call | solution.py:113
  13.9 2.6 %all-to-all-done = bf16[32,5,2,128]{3,2,1,0:T(2,128)(2,1)S(1)} async-done(((bf16[32,5,2,128]{3,2,1,0:T(2,128)(2,1)}), bf16[32,5,2,128]{3,2,1,0:T(2,128)(2,1)S(1)}, u32[]{:S(2)}, u32[]{:S(2)}) %all-to-all-start) | async-done | bytes 81952 | tf_op jit(solution)/shard_map/all_to_all | solution.py:700
  16.4 0.0 copy-done
  16.4 1.8 %assemble.1 = f32[2048,1024]{1,0:T(8,128)} custom-call(bf16[320,128]{1,0:T(8,128)(2,1)S(1)} %bitcast.5, f32[16,128]{1,0:T(8,128)S(1)} %bitcast.8, f32[2048,1024]{1,0:T(8,128)} %fill.1.filled_ref), custom_call_target="tpu_custom_call", output_to_operand_aliasing={{}: (2, {})} | custom-call | tf_op jit(solution)/shard_map/assemble/pallas_call | solution.py:654
Async XLA Ops:
  0.0 16.4 %copy-start = (f32[2048]{0:T(1024)S(1)}, f32[2048]{0:T(1024)}, u32[]{:S(2)}) copy-start(f32[2048]{0:T(1024)} %param.7) | copy-start | bytes 24580
  1.5 14.9 %all-to-all-start = ((bf16[32,5,2,128]{3,2,1,0:T(2,128)(2,1)}), bf16[32,5,2,128]{3,2,1,0:T(2,128)(2,1)S(1)}, u32[]{:S(2)}, u32[]{:S(2)}) async-start(bf16[32,5,2,128]{3,2,1,0:T(2,128)(2,1)} %bitcast.9), calls=%async_computation | async-start | bytes 163840 | tf_op jit(solution)/shard_map/all_to_all | solution.py:700
where the time goes:
time: 18.6 us; the launch traced here: 18.3 us
  Pallas kernels  8.36 us (45%)
  starting transfers between devices  7.33 us (39%)
  waiting for transfers between devices  2.56 us (14%)
    all_to_all x1, starting transfers between devices, body(): lax.all_to_all(packed, ('region', 'col'), split_axis=0, concat_axis=0, ti...  7.33 us
    pallas_call x1, Pallas kernels, fill(): pl.pallas_call(functools.partial(fill_kernel, place, (rows, cols)), out_s...  4.98 us
    all_to_all x1, waiting for transfers between devices, body(): lax.all_to_all(packed, ('region', 'col'), split_axis=0, concat_axis=0, ti...  2.56 us
    pallas_call x1, Pallas kernels, assemble(): pl.pallas_call(functools.partial(assemble_kernel, place, (rows, cols, chu...  1.84 us
    pallas_call x1, Pallas kernels, pack(): pl.pallas_call(functools.partial(pack_kernel, place), out_shape=jax.Shape...  1.54 us
  transfers between devices with their start and end apart: 1, of which 1 were waited for; matrix products, arithmetic and copies ran while one was open for 0% of the time, Pallas kernels for 27%

commit v1 on v0

--- a/solution.py
+++ b/solution.py
@@ -34,24 +34,39 @@
 
 
 SLOT = 10
+LABEL_AT = (0, 56, 64, 120)
 
 
 def pack_kernel(place, jac_ref, dest_ref, near_ref, prior_ref, out_ref):
     _, column = place()
-    lane = iota((1, 128), 1)
+    shape = (8, 128)
+    lane, row = iota(shape, 1), iota(shape, 0)
     fill_up = jnp.zeros((2, 120), f32)
     dest = jnp.concatenate([dest_ref[...].astype(f32), fill_up], axis=1)
     near = jnp.concatenate([near_ref[...].astype(f32), fill_up], axis=1)
-    line = dest[0:1, :] + pltpu.roll(near[0:1, :], 8, 1)
-    line = line + pltpu.roll(dest[1:2, :], 16, 1) + pltpu.roll(near[1:2, :], 24, 1)
+    labels = jnp.zeros(shape, f32)
+    for at, line in zip(LABEL_AT, (dest[0:1, :], near[0:1, :], dest[1:2, :], near[1:2, :])):
+        line = jnp.broadcast_to(line, shape)
+        labels = labels + (pltpu.roll(line, at, 1) if at else line)
     column = column % 8
-    prior = prior_ref[pl.ds(column // 4, 1), :]
-    prior = pltpu.roll(prior, (4 - column % 4) % 4 * 32, 1)
+    prior = jnp.broadcast_to(prior_ref[pl.ds(column // 4, 1), :], shape)
+    weights = jnp.zeros(shape, f32)
     for at, part in enumerate(split(prior, 3)):
-        moved = pltpu.roll(part.astype(f32), 32 * (at + 1), 1)
-        line = jnp.where(lane // 32 == at + 1, moved, line)
-    slot = jnp.concatenate([jac_ref[...].astype(f32), line, jnp.zeros((1, 128), f32)], axis=0)
-    eight = jnp.concatenate([slot] * 8, axis=0).astype(bf16)
+        moved = pltpu.roll(part.astype(f32), (4 + at - column % 4) % 4 * 32, 1)
+        weights = jnp.where(lane // 32 == at, moved, weights)
+    jac = jac_ref[...].astype(f32)
+    turned = [jac if not at else pltpu.roll(jac, 2 * at, 0) for at in range(4)]
+    pieces = []
+    for at in range(SLOT):
+        piece = jnp.zeros(shape, f32)
+        for slot in range(8):
+            first = SLOT * slot - 8 * at
+            if -SLOT < first < 8:
+                piece = jnp.where((row >= first) & (row < first + 8), turned[slot % 4], piece)
+                piece = jnp.where(row == first + 8, labels, piece)
+                piece = jnp.where(row == first + 9, weights, piece)
+        pieces.append(piece)
+    eight = jnp.concatenate(pieces, axis=0).astype(bf16)
     for at in range(out_ref.shape[0] // (8 * SLOT)):
         out_ref[8 * SLOT * at : 8 * SLOT * (at + 1), :] = eight
 
@@ -191,10 +206,13 @@
     return jnp.concatenate((by_rows + by_columns) * 2, axis=0).astype(bf16)
 
 
+def slot_rows(got_ref, a, at, per):
+    block = got_ref[pl.ds(a * (CH // 8) * SLOT, per * SLOT), :].astype(f32)
+    return jnp.concatenate([block[SLOT * d + at : SLOT * d + at + 1, :] for d in range(per)], axis=0)
+
+
 def label_rows(got_ref, a):
-    per = CH // 8
-    block = got_ref[pl.ds(a * per * SLOT, per * SLOT), :].astype(f32)
-    return jnp.concatenate([block[SLOT * d + 8 : SLOT * d + 9, :] for d in range(per)], axis=0)
+    return slot_rows(got_ref, a, 8, CH // 8)
 
 
 def jac_columns(got_ref, a):
@@ -206,16 +224,14 @@
 def spread(labels):
     lane8, row8 = iota((8, 128), 1), iota((8, 128), 0)
     out = []
-    for at in range(4):
+    for at in LABEL_AT:
         halves = []
         for half in range(2):
             total = jnp.zeros((8, 128), f32)
             for part in range(2):
                 from_row = 16 * half + 8 * part
                 piece = labels[from_row : from_row + 8, :]
-                if at:
-                    piece = pltpu.roll(piece, 128 - 8 * at, 1)
-                piece = pltpu.roll(piece, 64 * part, 1, stride=8, stride_axis=0)
+                piece = pltpu.roll(piece, (64 * part - at) % 128, 1, stride=8, stride_axis=0)
                 total = total + jnp.where(lane8 // 8 == row8 + 8 * part, piece, 0.0)
             halves.append(jnp.sum(total, axis=0, keepdims=True))
         out.append(jnp.concatenate(halves, axis=1))
@@ -246,49 +262,59 @@
     def measure(a):
         jac_t = jac_columns(got_ref, a)
         d0, n0, d1, n1 = spread(label_rows(got_ref, a))
-        here0 = d0 == 0
-        pose = jnp.where(here0, n0, n1) - column_f * col_poses
-        inside = (here0 | (d1 == 0)) & (pose >= 0) & (pose < col_poses)
-        pose = jnp.where(inside, pose, -1.0)
-        columns = to_columns(jnp.concatenate([pose, jnp.zeros((7, CH), f32)], axis=0))
-        j0, j1 = slabs(jac_t[0:64, :]), slabs(jac_t[64:128, :])
-        side = [jnp.where(here0, x, y) for x, y in zip(j0, j1)]
-        gram = jnp.concatenate(batched(side, side), axis=0)
-        of_pose = jnp.where(
-            columns[:, 0:1] == iota((CH, 128), 1).astype(f32), 1.0, 0.0
-        ).astype(bf16)
-        total = dot(jnp.concatenate(split(gram, 3), axis=0), of_pose)
+        grams, of_pose = [], []
+        for at, (region_of, number) in enumerate(((d0, n0), (d1, n1))):
+            side = slabs(jac_t[64 * at : 64 * at + 64, :])
+            gram = jnp.concatenate(batched(side, side), axis=0)
+            grams.append(jnp.concatenate(split(gram, 3), axis=0))
+            pose = number - column_f * col_poses
+            pose = jnp.where((region_of == 0) & (pose < col_poses), pose, -1.0)
+            of_pose.append(jnp.where(iota((128, CH), 0).astype(f32) == pose, 1.0, 0.0).astype(bf16))
+        total = dot(
+            jnp.concatenate(grams, axis=1), jnp.concatenate(of_pose, axis=1), ((1,), (1,))
+        )
         app[...] += total[0:64] + total[64:128] + total[128:192]
 
     loop(chunks, measure)
     gram = app[...]
     factor, _ = cholesky(slabs(gram + first))
-    lane, here = iota((64, 128), 1), jnp.where(column == 0, PP, 0)
-    in_panel = lane < here
-    both = [jnp.where(in_panel, 0.0, gram), jnp.where(in_panel, jnp.concatenate(factor, axis=0), 0.0)]
-    both = jnp.concatenate(both, axis=0).T
-    value = dot(jnp.concatenate(split(both, 2), axis=1), expansion())
-    pose, lane = iota((128, 128), 0), iota((128, 128), 1)
-    weights = [jnp.broadcast_to(local[at : at + 1, :], (16, 128)) for at in range(groups)]
-    weights += [jnp.zeros((16, 128), f32)] * (8 - groups)
-    weights = jnp.where(pose < here, 0.0, jnp.concatenate(weights, axis=0))
-    keep, lane_in, group_lane = lane // 8 == pose % 16, lane % 8, lane // 8
-    for k in range(8):
-        piece = jnp.where(keep, value[:, 128 * k : 128 * k + 128], 0.0)
-        piece = piece + jnp.where(keep & (lane_in == k), weights, 0.0)
-        squares[pl.ds(k, 128, stride=8), :] = piece
-    copies = [
-        pltpu.make_async_copy(
+    table = expansion()
+    by_rows, by_columns = table[0:64], table[64:128]
+
+    def copy_of(at):
+        return pltpu.make_async_copy(
             squares.at[pl.ds(at * 128, 128), :],
             out_ref.at[pl.ds(start + at * 128, 128), pl.ds(at * 128, 128)],
             sem.at[at],
         )
-        for at in range(groups)
-    ]
-    for copy in copies:
-        copy.start()
-    for copy in copies:
-        copy.wait()
+
+    def expanded(block, by, count):
+        full = jnp.concatenate([block, jnp.zeros((64, 128), f32)], axis=0).T[0:count, :]
+        high, low = (part[:, 0:64] for part in split(full, 2))
+        both = jnp.concatenate([high, low], axis=1)
+        return dot(both, jnp.concatenate([by, by], axis=0))
+
+    value = expanded(gram, by_rows, 128)
+    pose, lane = iota((128, 128), 0), iota((128, 128), 1)
+    weights = [jnp.broadcast_to(local[at : at + 1, :], (16, 128)) for at in range(groups)]
+    weights = jnp.concatenate(weights + [jnp.zeros((16, 128), f32)] * (8 - groups), axis=0)
+    keep, lane_in = lane // 8 == pose % 16, lane % 8
+    pieces = []
+    for k in range(8):
+        piece = jnp.where(keep, value[:, 128 * k : 128 * k + 128], 0.0)
+        piece = piece + jnp.where(keep & (lane_in == k), weights, 0.0)
+        pieces.append(piece[0:PP, :])
+        squares[pl.ds(PANEL + k, 128 - PP, stride=8), :] = piece[PP:, :]
+    for at in range(K_PANELS, groups):
+        copy_of(at).start()
+    value = expanded(jnp.concatenate(factor, axis=0), by_columns, PP)
+    for k in range(8):
+        piece = jnp.where(keep[0:PP, :], value[:, 128 * k : 128 * k + 128], 0.0)
+        squares[pl.ds(k, PP, stride=8), :] = jnp.where(column == 0, piece, pieces[k])
+    for at in range(K_PANELS):
+        copy_of(at).start()
+    for at in range(groups):
+        copy_of(at).wait()
 
 
 def general(place, sizes, got_ref, prior_ref, out_ref,
@@ -306,10 +332,10 @@
     table = expansion()
 
     labels0 = label_rows(got_ref, 0)
-    sent = labels0[0:8, :]
-    panel_prior = jnp.zeros((8, 128), f32)
-    for at in range(3):
-        panel_prior = panel_prior + pltpu.roll(sent, 128 - 32 * (at + 1), 1)
+    sent = slot_rows(got_ref, 0, 9, 8)
+    panel_prior = sent
+    for at in range(1, 3):
+        panel_prior = panel_prior + pltpu.roll(sent, 128 - 32 * at, 1)
     panel_prior = jnp.where(lane8 < 32, panel_prior, 0.0)
     lined = jnp.zeros((8, 128), f32)
     for at in range(4):

time: 18.6 us -> 18.3 us (0.984)
  Pallas kernels: 8.36 us -> 8.09 us
    pallas_call x1, Pallas kernels: 1.84 us -> 1.63 us  [assemble(): pl.pallas_call(functools.partial(assemble_kernel, place, (rows, cols, chu...]
  transfers between devices with their start and end apart: 1 -> 1, of which waited for: 1 -> 1; matrix products, arithmetic and copies ran while one was open for 0% -> 0% of each run, Pallas kernels for 27% -> 28%
where the time goes in v1:
time: 18.3 us; the launch traced here: 18 us
  Pallas kernels  8.09 us (44%)
  starting transfers between devices  7.33 us (40%)
  waiting for transfers between devices  2.56 us (14%)
    all_to_all x1, starting transfers between devices, body(): lax.all_to_all(packed, ('region', 'col'), split_axis=0, concat_axis=0, ti...  7.33 us
    pallas_call x1, Pallas kernels, fill(): pl.pallas_call(functools.partial(fill_kernel, place, (rows, cols)), out_s...  4.98 us
    all_to_all x1, waiting for transfers between devices, body(): lax.all_to_all(packed, ('region', 'col'), split_axis=0, concat_axis=0, ti...  2.56 us
    pallas_call x1, Pallas kernels, assemble(): pl.pallas_call(functools.partial(assemble_kernel, place, (rows, cols, chu...  1.63 us
    pallas_call x1, Pallas kernels, pack(): pl.pallas_call(functools.partial(pack_kernel, place), out_shape=jax.Shape...  1.48 us
  transfers between devices with their start and end apart: 1, of which 1 were waited for; matrix products, arithmetic and copies ran while one was open for 0% of the time, Pallas kernels for 28%

profile of v1, /device:TPU:0, one launch (start us, length us, event | category | flops | bytes accessed | tf_op | source)
XLA Modules:
  0.0 18.0 jit_solution(1597509381954675784)
XLA Ops:
  0.0 0.0 copy-start
  0.0 1.5 %pack.1 = bf16[320,128]{1,0:T(8,128)(2,1)} custom-call(bf16[8,128]{1,0:T(8,128)(2,1)} %jac_ref.1, s32[2,8]{1,0:T(2,128)} %bitcast.10, s32[2,8]{1,0:T(2,128)} %bitcast.11, f32[16,128]{1,0:T(8,128)} %bitcast.6), custom_call_target="tpu_custom_call" | custom-call | tf_op jit(solution)/shard_map/pack/pallas_call | solution.py:75
  1.5 7.3 %all-to-all-start = ((bf16[32,5,2,128]{3,2,1,0:T(2,128)(2,1)}), bf16[32,5,2,128]{3,2,1,0:T(2,128)(2,1)S(1)}, u32[]{:S(2)}, u32[]{:S(2)}) async-start(bf16[32,5,2,128]{3,2,1,0:T(2,128)(2,1)} %bitcast.9), calls=%async_computation | async-start | bytes 163840 | tf_op jit(solution)/shard_map/all_to_all | solution.py:726
  8.8 5.0 %fill.1.filled_ref = f32[2048,1024]{1,0:T(8,128)} custom-call(f32[16,128]{1,0:T(8,128)} %bitcast.7), custom_call_target="tpu_custom_call" | custom-call | bytes 8388608 | tf_op jit(solution)/shard_map/fill/pallas_call | solution.py:128
  13.8 2.6 %all-to-all-done = bf16[32,5,2,128]{3,2,1,0:T(2,128)(2,1)S(1)} async-done(((bf16[32,5,2,128]{3,2,1,0:T(2,128)(2,1)}), bf16[32,5,2,128]{3,2,1,0:T(2,128)(2,1)S(1)}, u32[]{:S(2)}, u32[]{:S(2)}) %all-to-all-start) | async-done | bytes 81952 | tf_op jit(solution)/shard_map/all_to_all | solution.py:726
  16.4 0.0 copy-done
  16.4 1.6 %assemble.1 = f32[2048,1024]{1,0:T(8,128)} custom-call(bf16[320,128]{1,0:T(8,128)(2,1)S(1)} %bitcast.5, f32[16,128]{1,0:T(8,128)S(1)} %bitcast.8, f32[2048,1024]{1,0:T(8,128)} %fill.1.filled_ref), custom_call_target="tpu_custom_call", output_to_operand_aliasing={{}: (2, {})} | custom-call | tf_op jit(solution)/shard_map/assemble/pallas_call | solution.py:680
Async XLA Ops:
  0.0 16.4 %copy-start = (f32[2048]{0:T(1024)S(1)}, f32[2048]{0:T(1024)}, u32[]{:S(2)}) copy-start(f32[2048]{0:T(1024)} %param.7) | copy-start | bytes 24580
  1.5 14.9 %all-to-all-start = ((bf16[32,5,2,128]{3,2,1,0:T(2,128)(2,1)}), bf16[32,5,2,128]{3,2,1,0:T(2,128)(2,1)S(1)}, u32[]{:S(2)}, u32[]{:S(2)}) async-start(bf16[32,5,2,128]{3,2,1,0:T(2,128)(2,1)} %bitcast.9), calls=%async_computation | async-start | bytes 163840 | tf_op jit(solution)/shard_map/all_to_all | solution.py:726
